TPU v7x, 32 devices: a whole 2x2x4 slice. The times are simulated.
32 devices in a mesh: blk: 8 (over z, x), rows: 4 (over y, core).
Axes of the slice: x: 2, y: 2, z: 4, core: 2. Of those that a mesh axis runs over, the one named last changes fastest.
Arguments:
- patterns: bfloat16 [2048, 4096], P('blk', 'rows'), may hold values from -6 to 6
- dictionary: bfloat16 [16384, 4096], P('blk', 'rows'), may hold values from -6 to 6
- codes: bfloat16 [2048, 256], P('blk'), may hold values from -6 to 6
- support: int32 [2048, 4], P('blk'), may hold values from 0 to 7, all different within a row
- wanted: int32 [8, 8], P('blk'), may hold values from 0 to 31
Outputs:
- dictionary_out: bfloat16 [16384, 4096], P('blk', 'rows')
- codes_out: float32 [2048, 256], P('blk')
Inputs may be any that keep to these rules, and one draw needn't show every extreme that they name: `support`: the 4 entries of a row are different, and every slot is named by some pattern.
All inputs are finite; a program needn't handle non-finite values.
Results may differ from a plain program's by a relative error of at most 0.014.
Values may be sent and summed in bfloat16 or wider, within the bound.
A program may use at most 64 MiB of HBM per device.

v0:
```python
import jax
import jax.numpy as jnp
from jax import lax
from jax.sharding import PartitionSpec as P

CODE_RATE = 0.05
ATOM_RATE = 0.2


def local(patterns, dictionary, codes, support, wanted):
    owners = lax.axis_size("blk")
    pattern_rows, pixel_count = patterns.shape
    support_count = support.shape[1]
    block_width = codes.shape[1] // support_count
    owned_blocks = dictionary.shape[0] // block_width
    scale_factor = (support_count * block_width) ** (-0.5)
    slot_ids = jnp.arange(owners, dtype=jnp.int32)
    picker = (support[:, :, None] == slot_ids[None, None, :]).astype(jnp.bfloat16)
    picker_wide = picker.astype(jnp.float32)
    asked = lax.all_to_all(wanted, "blk", split_axis=1, concat_axis=0, tiled=True)[:, 0]
    chooser = (asked[:, None] == jnp.arange(owned_blocks, dtype=jnp.int32)[None, :]).astype(
        jnp.float32
    )
    atoms_now = dictionary
    codes_now = codes
    for step_index in range(2):
        code_bf = codes_now.astype(jnp.bfloat16).reshape(pattern_rows, support_count, block_width)
        outgoing = jnp.take(
            atoms_now.reshape(owned_blocks, block_width, pixel_count), asked, axis=0
        )
        panels = lax.all_to_all(outgoing, "blk", split_axis=0, concat_axis=0, tiled=True)
        flat_panels = panels.reshape(owners * block_width, pixel_count)
        dense = jnp.einsum("psn,pse->pne", picker, code_bf, preferred_element_type=jnp.float32)
        dense = dense.astype(jnp.bfloat16).reshape(pattern_rows, owners * block_width)
        rebuilt = scale_factor * jnp.dot(dense, flat_panels, preferred_element_type=jnp.float32)
        residual = (patterns.astype(jnp.float32) - rebuilt).astype(jnp.bfloat16)
        correlated = lax.dot_general(
            residual, flat_panels, (((1,), (1,)), ((), ())), preferred_element_type=jnp.float32
        )
        code_terms = scale_factor * jnp.einsum(
            "psn,pne->pse",
            picker_wide,
            correlated.reshape(pattern_rows, owners, block_width),
            precision=lax.Precision.HIGHEST,
        )
        code_terms = code_terms.reshape(pattern_rows, support_count * block_width)
        atom_terms = scale_factor * lax.dot_general(
            dense, residual, (((0,), (0,)), ((), ())), preferred_element_type=jnp.float32
        )
        code_share = lax.psum_scatter(
            code_terms.astype(jnp.bfloat16), "rows", scatter_dimension=0, tiled=True
        ).astype(jnp.float32)
        share_rows = code_share.shape[0]
        first_row = lax.axis_index("rows") * share_rows
        own_codes = lax.dynamic_slice_in_dim(
            codes_now.astype(jnp.float32), first_row, share_rows, 0
        )
        codes_now = lax.all_gather(own_codes + CODE_RATE * code_share, "rows", axis=0, tiled=True)
        arrived = lax.all_to_all(
            atom_terms.reshape(owners, block_width, pixel_count),
            "blk",
            split_axis=0,
            concat_axis=0,
            tiled=True,
        )
        atom_grad = jnp.einsum("nb,nex->bex", chooser, arrived, precision=lax.Precision.HIGHEST)
        atoms_now = (
            atoms_now.astype(jnp.float32)
            + ATOM_RATE * atom_grad.reshape(owned_blocks * block_width, pixel_count)
        ).astype(jnp.bfloat16)
    return (atoms_now, codes_now)


def solution(mesh):
    placed = (P("blk", "rows"), P("blk", "rows"), P("blk", None), P("blk", None), P("blk", None))
    return jax.shard_map(
        local,
        mesh=mesh,
        in_specs=placed,
        out_specs=(P("blk", "rows"), P("blk", None)),
        check_vma=False,
    )
```

profile of v0, /device:TPU:0, one launch (start us, length us, event | category | flops | bytes accessed | tf_op | source)
XLA Modules:
  0.0 240.9 jit_solution(2206172813161173599)
XLA Ops:
  7.2 0.8 copy.72
  8.0 13.6 %all_to_all.33 = s32[1,8,1]{2,0,1:T(1,128)S(1)} all-to-all(s32[1,8,1]{2,0,1:T(1,128)S(1)} %copy.72), channel_id=1, replica_groups=mesh['blk'=8,'rows'=4] {'blk'}, dimensions={1} | all-to-all | bytes 64 | tf_op jit(solution)/shard_map/all_to_all | solution.py:20
  21.5 0.2 reduce
  21.8 2.8 %gather_fusion = bf16[8,64,1024]{2,1,0:T(8,128)(2,1)S(1)} fusion(bf16[32,64,1024]{2,1,0:T(8,128)(2,1)} %bitcast.63, s32[1024]{0:T(1024)S(1)} %pad_clamp_fusion), kind=kCustom, calls=%fused_computation.clone | custom fusion | bytes 2097184 | tf_op jit(solution)/shard_map/jit(_take)/gather | solution.py:28
  24.6 1.1 broadcast_select_fusion.1
  25.7 3.6 %all-to-all-start.1 = ((bf16[8,64,1024]{2,1,0:T(8,128)(2,1)}), bf16[8,64,1024]{2,1,0:T(8,128)(2,1)S(1)}, u32[]{:S(2)}, u32[]{:S(2)}) async-start(bf16[8,64,1024]{2,1,0:T(8,128)(2,1)} %broadcast_select_fusion.1), calls=%async_computation.1 | async-start | bytes 2097152 | tf_op jit(solution)/shard_map/all_to_all | solution.py:31
  29.3 0.1 copy.73
  29.6 0.2 copy.75
  29.8 0.9 fusion.17
  30.6 0.3 copy.76
  31.0 23.1 %all-to-all-done.1 = bf16[8,64,1024]{2,1,0:T(8,128)(2,1)S(1)} async-done(((bf16[8,64,1024]{2,1,0:T(8,128)(2,1)}), bf16[8,64,1024]{2,1,0:T(8,128)(2,1)S(1)}, u32[]{:S(2)}, u32[]{:S(2)}) %all-to-all-start.1) | async-done | bytes 1048608 | tf_op jit(solution)/shard_map/all_to_all | solution.py:31
  54.0 0.5 fusion.9
  54.5 0.4 convolution_multiply_fusion.1
  54.9 51.6 %all_to_all.34 = f32[8,64,1024]{2,1,0:T(8,128)S(1)} all-to-all(f32[8,64,1024]{2,1,0:T(8,128)S(1)} %bitcast.62), channel_id=1, replica_groups=mesh['blk'=8,'rows'=4] {'blk'}, dimensions={0} | all-to-all | bytes 4194304 | tf_op jit(solution)/shard_map/all_to_all | solution.py:59
  106.5 4.1 %broadcast_multiply_fusion.1 = f32[32,64,1024]{2,0,1:T(8,128)S(1)} fusion(f32[8,64,1024]{2,1,0:T(8,128)S(1)} %all_to_all.34, s32[8]{0:T(128)S(1)} %reduce), kind=kOutput, calls=%fused_computation.7 | convolution fusion | flops 203424000 | bytes 10485792 | tf_op jit(solution)/shard_map/nb,nex->bex/dot_general | solution.py:66
  110.6 4.9 %copy.78 = f32[32,64,1024]{2,1,0:T(8,128)S(1)} copy(f32[32,64,1024]{2,0,1:T(8,128)S(1)} %broadcast_multiply_fusion.1) | data formatting | bytes 16777216 | tf_op jit(solution)/shard_map/mul | solution.py:69
  115.5 6.8 %fusion.1 = bf16[2048,1024]{1,0:T(8,128)(2,1)} fusion(f32[32,64,1024]{2,1,0:T(8,128)S(1)} %copy.78, bf16[2048,1024]{1,0:T(8,128)(2,1)} %param.8), kind=kLoop, calls=%fused_computation.5 | loop fusion | flops 6291456 | bytes 16777216 | tf_op jit(solution)/shard_map/convert_element_type | solution.py:70
  122.3 2.8 %gather_fusion.1 = bf16[8,64,1024]{2,1,0:T(8,128)(2,1)S(1)} fusion(bf16[32,64,1024]{2,1,0:T(8,128)(2,1)} %bitcast.61, s32[1024]{0:T(1024)S(1)} %pad_clamp_fusion), kind=kCustom, calls=%fused_computation.1.clone | custom fusion | bytes 2097184 | tf_op jit(solution)/shard_map/jit(_take)/gather | solution.py:28
  125.1 1.3 broadcast_select_fusion
  126.4 3.6 %all-to-all-start.3 = ((bf16[8,64,1024]{2,1,0:T(8,128)(2,1)}), bf16[8,64,1024]{2,1,0:T(8,128)(2,1)S(1)}, u32[]{:S(2)}, u32[]{:S(2)}) async-start(bf16[8,64,1024]{2,1,0:T(8,128)(2,1)} %broadcast_select_fusion), calls=%async_computation.3 | async-start | bytes 2097152 | tf_op jit(solution)/shard_map/all_to_all | solution.py:31
  130.1 0.5 fusion.12
  130.6 0.4 copy.80
  131.0 1.1 fusion.16
  132.1 0.2 copy.81
  132.3 0.8 copy.92
  133.1 21.9 %reduce-scatter.7.cloned.1.call-done = bf16[64,256]{1,0:T(8,128)(2,1)} async-done(((bf16[256,256]{1,0:T(8,128)(2,1)}), bf16[64,256]{1,0:T(8,128)(2,1)}) %reduce-scatter.7.cloned.1.call-update) | async-done | bytes 32784
  155.0 0.9 copy.93
  156.0 5.8 %all_gather.6 = f32[256,256]{1,0:T(8,128)S(1)} all-gather(f32[64,256]{1,0:T(8,128)S(1)} %copy.82), channel_id=1, replica_groups=mesh['blk'=8,'rows'=4] {'rows'}, dimensions={0}, use_global_device_ids=true | all-gather | bytes 327680 | tf_op jit(solution)/shard_map/all_gather | solution.py:58
  162.0 0.2 copy.84
  162.2 0.9 fusion.15
  163.0 0.3 copy.85
  163.4 0.5 fusion.8
  163.9 0.8 copy-done.1
  164.7 1.8 convolution_multiply_fusion
  166.4 5.5 %all-to-all-start.4 = ((f32[8,64,1024]{2,1,0:T(8,128)}), f32[8,64,1024]{2,1,0:T(8,128)S(1)}, u32[]{:S(2)}, u32[]{:S(2)}) async-start(f32[8,64,1024]{2,1,0:T(8,128)} %bitcast.14), calls=%async_computation.4 | async-start | bytes 4194304 | tf_op jit(solution)/shard_map/all_to_all | solution.py:59
  172.0 2.3 fusion.10
  174.3 1.5 copy.89
  175.8 1.9 fusion.14
  177.7 1.2 copy.90
  178.9 0.8 copy.94
  179.7 20.2 %reduce-scatter.9.cloned.1.call-done = bf16[64,256]{1,0:T(8,128)(2,1)} async-done(((bf16[256,256]{1,0:T(8,128)(2,1)}), bf16[64,256]{1,0:T(8,128)(2,1)}) %reduce-scatter.9.cloned.1.call-update) | async-done | bytes 32784
  199.9 0.9 copy.95
  201.0 6.0 %all_gather.7 = f32[256,256]{1,0:T(8,128)S(1)} all-gather(f32[64,256]{1,0:T(8,128)S(1)} %copy.91), channel_id=1, replica_groups=mesh['blk'=8,'rows'=4] {'rows'}, dimensions={0}, use_global_device_ids=true | all-gather | bytes 327680 | tf_op jit(solution)/shard_map/all_gather | solution.py:58
  207.1 13.7 %all-to-all-done.4 = f32[8,64,1024]{2,1,0:T(8,128)S(1)} async-done(((f32[8,64,1024]{2,1,0:T(8,128)}), f32[8,64,1024]{2,1,0:T(8,128)S(1)}, u32[]{:S(2)}, u32[]{:S(2)}) %all-to-all-start.4) | async-done | bytes 2097184 | tf_op jit(solution)/shard_map/all_to_all | solution.py:59
  220.7 4.1 %broadcast_multiply_fusion = f32[32,64,1024]{2,0,1:T(8,128)S(1)} fusion(f32[8,64,1024]{2,1,0:T(8,128)S(1)} %all-to-all-done.4, s32[8]{0:T(128)S(1)} %reduce), kind=kOutput, calls=%fused_computation.6 | convolution fusion | flops 203424000 | bytes 10485792 | tf_op jit(solution)/shard_map/nb,nex->bex/dot_general | solution.py:66
  224.8 4.9 %copy.87 = f32[32,64,1024]{2,1,0:T(8,128)S(1)} copy(f32[32,64,1024]{2,0,1:T(8,128)S(1)} %broadcast_multiply_fusion) | data formatting | bytes 16777216 | tf_op jit(solution)/shard_map/mul | solution.py:69
  229.7 3.7 %fusion = bf16[2048,1024]{1,0:T(8,128)(2,1)} fusion(f32[32,64,1024]{2,1,0:T(8,128)S(1)} %copy.87, bf16[2048,1024]{1,0:T(8,128)(2,1)S(1)} %copy-done), kind=kLoop, calls=%fused_computation.3 | loop fusion | flops 6291456 | bytes 16777216 | tf_op jit(solution)/shard_map/convert_element_type | solution.py:70
  233.4 0.7 copy.101
  (28 shorter events, 0.8 us)
Async XLA Ops:
  7.2 22.1 %copy-start.3 = (s32[256,4]{0,1:T(4,128)S(1)}, s32[256,4]{0,1:T(4,128)}, u32[]{:S(2)}) copy-start(s32[256,4]{0,1:T(4,128)} %param.10) | copy-start | bytes 12292
  7.2 22.3 %copy-start.2 = (bf16[256,256]{1,0:T(8,128)(2,1)S(1)}, bf16[256,256]{1,0:T(8,128)(2,1)}, u32[]{:S(2)}) copy-start(bf16[256,256]{1,0:T(8,128)(2,1)} %param.9) | copy-start | bytes 393220
  24.6 29.4 %copy-start.4 = (bf16[256,1024]{1,0:T(8,128)(2,1)S(1)}, bf16[256,1024]{1,0:T(8,128)(2,1)}, u32[]{:S(2)}) copy-start(bf16[256,1024]{1,0:T(8,128)(2,1)} %param.7) | copy-start | bytes 1572868
  25.7 28.3 %all-to-all-start.1 = ((bf16[8,64,1024]{2,1,0:T(8,128)(2,1)}), bf16[8,64,1024]{2,1,0:T(8,128)(2,1)S(1)}, u32[]{:S(2)}, u32[]{:S(2)}) async-start(bf16[8,64,1024]{2,1,0:T(8,128)(2,1)} %broadcast_select_fusion.1), calls=%async_computation.1 | async-start | bytes 2097152 | tf_op jit(solution)/shard_map/all_to_all | solution.py:31
  126.4 36.9 %all-to-all-start.3 = ((bf16[8,64,1024]{2,1,0:T(8,128)(2,1)}), bf16[8,64,1024]{2,1,0:T(8,128)(2,1)S(1)}, u32[]{:S(2)}, u32[]{:S(2)}) async-start(bf16[8,64,1024]{2,1,0:T(8,128)(2,1)} %broadcast_select_fusion), calls=%async_computation.3 | async-start | bytes 2097152 | tf_op jit(solution)/shard_map/all_to_all | solution.py:31
  130.1 24.9 %reduce-scatter.7.cloned.1.call-start = ((), (), s32[]{:S(2)}) async-start(), calls=%async_computation.7 | async-start | bytes 163840
  131.0 32.4 %copy-start.5 = (bf16[256,1024]{1,0:T(8,128)(2,1)S(1)}, bf16[256,1024]{1,0:T(8,128)(2,1)}, u32[]{:S(2)}) copy-start(bf16[256,1024]{1,0:T(8,128)(2,1)} %param.7) | copy-start | bytes 1572868
  163.9 0.8 copy-start.1
  166.4 54.3 %all-to-all-start.4 = ((f32[8,64,1024]{2,1,0:T(8,128)}), f32[8,64,1024]{2,1,0:T(8,128)S(1)}, u32[]{:S(2)}, u32[]{:S(2)}) async-start(f32[8,64,1024]{2,1,0:T(8,128)} %bitcast.14), calls=%async_computation.4 | async-start | bytes 4194304 | tf_op jit(solution)/shard_map/all_to_all | solution.py:59
  172.0 28.0 %reduce-scatter.9.cloned.1.call-start = ((), (), s32[]{:S(2)}) async-start(), calls=%async_computation.8 | async-start | bytes 163840
  224.8 4.9 %copy-start = (bf16[2048,1024]{1,0:T(8,128)(2,1)S(1)}, bf16[2048,1024]{1,0:T(8,128)(2,1)}, u32[]{:S(2)}) copy-start(bf16[2048,1024]{1,0:T(8,128)(2,1)} %fusion.1) | copy-start | bytes 12582916
Sparse Core Ops, SparseCore 0:
  133.9 21.0 reduce-scatter.6
  179.8 20.0 reduce-scatter.8
where the time goes:
time: 242 us; the launch traced here: 241 us
  waiting for transfers between devices  78.8 us (33%)
  blocking collectives  77 us (32%)
  local copies, waits for them, and re-layouts  25.7 us (11%)
  matrix products  18.8 us (8%)
  between operations  14.4 us (6%)
  other arithmetic  13.5 us (6%)
  starting transfers between devices  12.8 us (5%)
    all_to_all x1, blocking collectives, local(): lax.all_to_all(atom_terms.reshape(owners, block_width, pixel_count), 'blk...  51.6 us
    unnamed x4, waiting for transfers between devices  42.1 us
    all_to_all x2, waiting for transfers between devices, local(): lax.all_to_all(outgoing, 'blk', split_axis=0, concat_axis=0, tiled=True)  23.1 us
    all_to_all x1, waiting for transfers between devices, local(): lax.all_to_all(atom_terms.reshape(owners, block_width, pixel_count), 'blk...  13.7 us
    all_to_all x1, blocking collectives, local(): lax.all_to_all(wanted, 'blk', split_axis=1, concat_axis=0, tiled=True)[:, 0]  13.6 us
    all_gather x2, blocking collectives, local(): lax.all_gather(own_codes + CODE_RATE * code_share, 'rows', axis=0, tiled=...  11.8 us
    convert_element_type x2, other arithmetic, local(): atoms_now = (atoms_now.astype(jnp.float32) + ATOM_RATE * atom_grad.reshap...  10.5 us
    mul x2, local copies, waits for them, and re-layouts, local(): ATOM_RATE * atom_grad.reshape(owned_blocks * block_width, pixel_count)  9.71 us
  transfers between devices with their start and end apart: 5, of which 4 were waited for; matrix products, arithmetic and copies ran while one was open for 7% of the time, Pallas kernels for 0%

commit v1 on v0

v1 whole, which is shorter than its diff:
```python
import functools

import jax
import jax.numpy as jnp
from jax import lax
from jax.experimental import pallas as pl
from jax.experimental.pallas import tpu as pltpu
from jax.sharding import PartitionSpec as P

CODE_RATE = 0.05
ATOM_RATE = 0.2
CHUNK = 256
MESH = pl.DeviceIdType.MESH


def steps_kernel(
    owners, row_count, block_width, chunk, scale_factor,
    same_ref, support_ref, codes_ref, patterns_ref, slots_ref,
    slots_out, codes_out,
    panels, arrived, terms, slots_next, dense, correlated, code_parts,
    send_sems, recv_sems, code_send, code_recv,
):
    me = lax.axis_index("blk")
    my_row = lax.axis_index("rows")
    pattern_rows, pixel_count = patterns_ref.shape
    chunks = pixel_count // chunk
    support_count = support_ref.shape[1]
    lanes = 128
    per_lane = lanes // block_width

    barrier = pltpu.get_barrier_semaphore()
    for j in range(1, owners):
        pl.semaphore_signal(
            barrier, inc=1, device_id={"blk": lax.rem(me + j, owners)}, device_id_type=MESH
        )
    for j in range(1, row_count):
        pl.semaphore_signal(
            barrier, inc=1, device_id={"rows": lax.rem(my_row + j, row_count)}, device_id_type=MESH
        )
    pl.semaphore_wait(barrier, owners + row_count - 2)

    def columns(k):
        return pl.ds(pl.multiple_of(k * chunk, chunk), chunk)

    def block_copy(phase, k, j, source, target):
        return pltpu.make_async_remote_copy(
            src_ref=source,
            dst_ref=target,
            send_sem=send_sems.at[phase, k, j],
            recv_sem=recv_sems.at[phase, k, j],
            device_id={"blk": lax.rem(me + j, owners)},
            device_id_type=MESH,
        )

    def wait_arrivals(phase, k, target):
        for j in range(1, owners):
            block_copy(phase, k, j, target, target).wait_recv()

    def send_panels(k, _):
        for j in range(1, owners):
            block_copy(
                0, k, j,
                slots_ref.at[lax.rem(me + j, owners), :, columns(k)],
                panels.at[0, k, me],
            ).start()
        panels[0, k, me] = slots_ref[me, :, columns(k)]
        return 0

    lax.fori_loop(0, chunks, send_panels, 0)

    half = lax.broadcasted_iota(jnp.int32, (pattern_rows, lanes), 1) // block_width

    def matches(s, m):
        return support_ref[:, s:s + 1] == half + m * per_lane

    def spread(codes_now):
        pieces = []
        for s in range(support_count):
            piece = codes_now[:, s * block_width:(s + 1) * block_width]
            pieces.append(jnp.concatenate([piece] * per_lane, axis=1))
        for m in range(owners // per_lane):
            total = jnp.zeros((pattern_rows, lanes), jnp.float32)
            for s in range(support_count):
                total = jnp.where(matches(s, m), pieces[s], total)
            dense[:, m * lanes:(m + 1) * lanes] = total.astype(jnp.bfloat16)

    def pick():
        pieces = []
        for s in range(support_count):
            total = jnp.zeros((pattern_rows, lanes), jnp.float32)
            for m in range(owners // per_lane):
                total = jnp.where(matches(s, m), correlated[:, m * lanes:(m + 1) * lanes], total)
            folded = total[:, :block_width]
            for h in range(1, per_lane):
                folded = folded + total[:, h * block_width:(h + 1) * block_width]
            pieces.append(folded)
        return scale_factor * jnp.concatenate(pieces, axis=1)

    def code_copy(step, j):
        return pltpu.make_async_remote_copy(
            src_ref=code_parts.at[step, my_row],
            dst_ref=code_parts.at[step, my_row],
            send_sem=code_send.at[step, j],
            recv_sem=code_recv.at[step, j],
            device_id={"rows": lax.rem(my_row + j, row_count)},
            device_id_type=MESH,
        )

    codes_out[...] = codes_ref[...].astype(jnp.float32)

    for step in range(2):
        spread(codes_out[...].astype(jnp.bfloat16).astype(jnp.float32))
        correlated[...] = jnp.zeros_like(correlated)

        def region_chunk(k, _, step=step):
            wait_arrivals(2 * step, k, panels.at[step, k, 0])
            panel = panels[step, k].reshape(owners * block_width, chunk)
            coefficients = dense[...]
            rebuilt = scale_factor * jnp.dot(
                coefficients, panel, preferred_element_type=jnp.float32
            )
            residual = (patterns_ref[:, columns(k)].astype(jnp.float32) - rebuilt).astype(
                jnp.bfloat16
            )
            atom_terms = scale_factor * lax.dot_general(
                coefficients, residual, (((0,), (0,)), ((), ())),
                preferred_element_type=jnp.float32,
            )
            terms[step, k] = atom_terms.astype(jnp.bfloat16).reshape(owners, block_width, chunk)
            for j in range(1, owners):
                block_copy(
                    2 * step + 1, k, j,
                    terms.at[step, k, lax.rem(me + j, owners)],
                    arrived.at[step, k, me],
                ).start()
            arrived[step, k, me] = terms[step, k, me]
            correlated[...] += lax.dot_general(
                residual, panel, (((1,), (1,)), ((), ())), preferred_element_type=jnp.float32
            )
            return 0

        lax.fori_loop(0, chunks, region_chunk, 0)
        code_parts[step, my_row] = pick().astype(jnp.bfloat16)
        for j in range(1, row_count):
            code_copy(step, j).start()

        def owner_chunk(k, _, step=step):
            wait_arrivals(2 * step + 1, k, arrived.at[step, k, 0])

            def one_slot(r, _):
                total = jnp.zeros((block_width, chunk), jnp.float32)
                for q in range(owners):
                    total = total + same_ref[r, q] * arrived[step, k, q].astype(jnp.float32)
                before = slots_ref[r, :, columns(k)] if step == 0 else slots_next[k, r]
                after = (before.astype(jnp.float32) + ATOM_RATE * total).astype(jnp.bfloat16)
                if step == 0:
                    slots_next[k, r] = after
                else:
                    slots_out[r, :, columns(k)] = after
                return 0

            lax.fori_loop(0, owners, one_slot, 0)
            if step == 0:
                for j in range(1, owners):
                    block_copy(
                        2, k, j,
                        slots_next.at[k, lax.rem(me + j, owners)],
                        panels.at[1, k, me],
                    ).start()
                panels[1, k, me] = slots_next[k, me]
            return 0

        lax.fori_loop(0, chunks, owner_chunk, 0)
        for j in range(1, row_count):
            code_copy(step, j).wait_recv()
        total = code_parts[step, 0].astype(jnp.float32)
        for i in range(1, row_count):
            total = total + code_parts[step, i].astype(jnp.float32)
        codes_out[...] += CODE_RATE * total

    def drain(k, _):
        for phase in range(4):
            for j in range(1, owners):
                block_copy(phase, k, j, terms.at[0, k, 0], terms.at[0, k, 0]).wait_send()
        return 0

    lax.fori_loop(0, chunks, drain, 0)
    for step in range(2):
        for j in range(1, row_count):
            code_copy(step, j).wait_send()


def put_kernel(group, selected_ref, dictionary_ref, slots_ref, out_ref):
    first = pl.program_id(0) * group
    for i in range(group):
        chosen = selected_ref[first + i]

        @pl.when(chosen >= 0)
        def _():
            out_ref[i] = slots_ref[jnp.maximum(chosen, 0)]

        @pl.when(chosen < 0)
        def _():
            out_ref[i] = dictionary_ref[i]


def local(patterns, dictionary, codes, support, wanted):
    owners = lax.axis_size("blk")
    row_count = lax.axis_size("rows")
    pattern_rows, pixel_count = patterns.shape
    support_count = support.shape[1]
    code_width = codes.shape[1]
    block_width = code_width // support_count
    owned_blocks = dictionary.shape[0] // block_width
    scale_factor = code_width ** (-0.5)
    chunk = min(CHUNK, pixel_count)
    chunks = pixel_count // chunk
    asked = lax.all_to_all(wanted, "blk", split_axis=1, concat_axis=0, tiled=True)[:, 0]
    same = (asked[:, None] == asked[None, :]).astype(jnp.float32)
    blocks = dictionary.reshape(owned_blocks, block_width, pixel_count)
    slots = jnp.take(blocks, asked, axis=0)
    vmem = pl.BlockSpec(memory_space=pltpu.VMEM)
    bf16 = jnp.bfloat16
    slots_after, codes_after = pl.pallas_call(
        functools.partial(steps_kernel, owners, row_count, block_width, chunk, scale_factor),
        out_shape=(
            jax.ShapeDtypeStruct((owners, block_width, pixel_count), bf16),
            jax.ShapeDtypeStruct((pattern_rows, code_width), jnp.float32),
        ),
        in_specs=[pl.BlockSpec(memory_space=pltpu.SMEM)] + [vmem] * 4,
        out_specs=(vmem, vmem),
        scratch_shapes=[
            pltpu.VMEM((2, chunks, owners, block_width, chunk), bf16),
            pltpu.VMEM((2, chunks, owners, block_width, chunk), bf16),
            pltpu.VMEM((2, chunks, owners, block_width, chunk), bf16),
            pltpu.VMEM((chunks, owners, block_width, chunk), bf16),
            pltpu.VMEM((pattern_rows, owners * block_width), bf16),
            pltpu.VMEM((pattern_rows, owners * block_width), jnp.float32),
            pltpu.VMEM((2, row_count, pattern_rows, code_width), bf16),
            pltpu.SemaphoreType.DMA((4, chunks, owners)),
            pltpu.SemaphoreType.DMA((4, chunks, owners)),
            pltpu.SemaphoreType.DMA((2, row_count)),
            pltpu.SemaphoreType.DMA((2, row_count)),
        ],
        compiler_params=pltpu.CompilerParams(
            collective_id=0, has_side_effects=True, vmem_limit_bytes=40 * 1024 * 1024
        ),
    )(same, support, codes, patterns, slots)
    slot_ids = jnp.arange(owners, dtype=jnp.int32)
    block_ids = jnp.arange(owned_blocks, dtype=jnp.int32)
    selected = jnp.max(
        jnp.where(asked[None, :] == block_ids[:, None], slot_ids[None, :], -1), axis=1
    )
    group = 4
    dictionary_after = pl.pallas_call(
        functools.partial(put_kernel, group),
        out_shape=jax.ShapeDtypeStruct(blocks.shape, bf16),
        grid_spec=pltpu.PrefetchScalarGridSpec(
            num_scalar_prefetch=1,
            grid=(owned_blocks // group,),
            in_specs=[
                pl.BlockSpec((group, block_width, pixel_count), lambda i, sel: (i, 0, 0)),
                pl.BlockSpec((owners, block_width, pixel_count), lambda i, sel: (0, 0, 0)),
            ],
            out_specs=pl.BlockSpec((group, block_width, pixel_count), lambda i, sel: (i, 0, 0)),
        ),
    )(selected, blocks, slots_after)
    return (dictionary_after.reshape(dictionary.shape), codes_after)


def solution(mesh):
    placed = (P("blk", "rows"), P("blk", "rows"), P("blk", None), P("blk", None), P("blk", None))
    return jax.shard_map(
        local,
        mesh=mesh,
        in_specs=placed,
        out_specs=(P("blk", "rows"), P("blk", None)),
        check_vma=False,
    )
```

time: 242 us -> 125 us (0.52)
  Pallas kernels: 0 us -> 103 us
  blocking collectives: 77 us -> 0 us
  waiting for transfers between devices: 78.8 us -> 5.6 us
  local copies, waits for them, and re-layouts: 25.7 us -> 6.69 us
  matrix products: 18.8 us -> 0 us
  between operations: 14.4 us -> 0.71 us
  other arithmetic: 13.5 us -> 1.08 us
  starting transfers between devices: 12.8 us -> 7.28 us
    pallas_call x0 -> x2, Pallas kernels: none -> 103 us  [the longest x1 95.6 us: local(): pl.pallas_call(functools.partial(steps_kernel, owners, row_count, block_w...]
    all_to_all x2 -> x0, blocking collectives: 65.2 us -> none  [the longest x1 51.6 us: local(): lax.all_to_all(atom_terms.reshape(owners, block_width, pixel_count), 'blk...]
    unnamed x4 -> x0, waiting for transfers between devices: 42.1 us -> none
    all_to_all x3 -> x1, waiting for transfers between devices: 36.7 us -> 5.6 us  [local(): lax.all_to_all(wanted, 'blk', split_axis=1, concat_axis=0, tiled=True)[:, 0]]
    dot_general x12 -> x0, matrix products: 18.8 us -> none  [the longest x2 8.16 us: local(): jnp.einsum('nb,nex->bex', chooser, arrived, precision=lax.Precision.HIGHEST)]
    all_gather x2 -> x0, blocking collectives: 11.8 us -> none  [local(): lax.all_gather(own_codes + CODE_RATE * code_share, 'rows', axis=0, tiled=...]
    convert_element_type x5 -> x1, other arithmetic: 10.6 us -> 0.07 us  [local(): same = (asked[:, None] == asked[None, :]).astype(jnp.float32)]
    mul x2 -> x0, local copies, waits for them, and re-layouts: 9.71 us -> none  [local(): ATOM_RATE * atom_grad.reshape(owned_blocks * block_width, pixel_count)]
  transfers between devices with their start and end apart: 5 -> 1, of which waited for: 4 -> 1; matrix products, arithmetic and copies ran while one was open for 7% -> 1% of each run, Pallas kernels for 0% -> 0%
where the time goes in v1:
time: 125 us
  Pallas kernels  103 us (82%)
  starting transfers between devices  7.28 us (6%)
  local copies, waits for them, and re-layouts  6.69 us (5%)
  waiting for transfers between devices  5.6 us (4%)
    pallas_call x1, Pallas kernels, local(): pl.pallas_call(functools.partial(steps_kernel, owners, row_count, block_w...  95.6 us
    pallas_call x1, Pallas kernels, local(): pl.pallas_call(functools.partial(put_kernel, group), out_shape=jax.ShapeD...  7.69 us
    all_to_all x1, starting transfers between devices, local(): lax.all_to_all(wanted, 'blk', split_axis=1, concat_axis=0, tiled=True)[:, 0]  7.28 us
    all_to_all x1, waiting for transfers between devices, local(): lax.all_to_all(wanted, 'blk', split_axis=1, concat_axis=0, tiled=True)[:, 0]  5.6 us
    gather x1, local copies, waits for them, and re-layouts, local(): slots = jnp.take(blocks, asked, axis=0)  2.8 us
    unnamed x8, local copies, waits for them, and re-layouts  2.5 us
  transfers between devices with their start and end apart: 1, of which 1 were waited for; matrix products, arithmetic and copies ran while one was open for 1% of the time, Pallas kernels for 0%

profile of v1, /device:TPU:0, one launch (start us, length us, event | category | flops | bytes accessed | tf_op | source)
XLA Modules:
  0.0 124.7 jit_solution(10465370248526399623)
XLA Ops:
  0.6 0.0 copy-start.2
  0.6 0.0 copy-start.1
  0.6 1.4 %copy.12 = s32[1,8,1]{2,0,1:T(1,128)} copy(s32[1,8,1]{1,2,0:T(1,128)} %bitcast.10) | data formatting | bytes 64 | tf_op jit(solution)/shard_map/all_to_all | solution.py:218
  2.0 7.3 %all-to-all-start = ((s32[1,8,1]{2,0,1:T(1,128)}), s32[1,8,1]{2,0,1:T(1,128)S(1)}, u32[]{:S(2)}, u32[]{:S(2)}) async-start(s32[1,8,1]{2,0,1:T(1,128)} %copy.12), calls=%async_computation | async-start | bytes 8192 | tf_op jit(solution)/shard_map/all_to_all | solution.py:218
  9.3 0.8 copy.13.support_ref
  10.1 5.6 %all-to-all-done = s32[1,8,1]{2,0,1:T(1,128)S(1)} async-done(((s32[1,8,1]{2,0,1:T(1,128)}), s32[1,8,1]{2,0,1:T(1,128)S(1)}, u32[]{:S(2)}, u32[]{:S(2)}) %all-to-all-start) | async-done | bytes 64 | tf_op jit(solution)/shard_map/all_to_all | solution.py:218
  15.7 0.2 reduce
  16.0 0.6 select_reduce_fusion.selected_ref
  16.6 0.1 compare_convert_fusion.same_ref
  16.7 2.8 %gather_fusion = bf16[8,64,1024]{2,1,0:T(8,128)(2,1)S(1)} fusion(bf16[32,64,1024]{2,1,0:T(8,128)(2,1)} %bitcast.7, s32[1024]{0:T(1024)S(1)} %pad_clamp_fusion), kind=kCustom, calls=%fused_computation | custom fusion | bytes 2097184 | tf_op jit(solution)/shard_map/jit(_take)/gather | solution.py:221
  19.5 0.2 broadcast_select_fusion.slots_ref
  19.6 0.0 copy-done.2
  19.7 0.0 copy-done.1
  19.7 95.6 %shard_map.68 = (bf16[8,64,1024]{2,1,0:T(8,128)(2,1)S(1)}, f32[256,256]{1,0:T(8,128)S(1)}) custom-call(f32[8,8]{1,0:T(8,128)S(1)} %compare_convert_fusion.same_ref, s32[256,4]{1,0:T(8,128)S(1)} %copy.13.support_ref, bf16[256,256]{1,0:T(8,128)(2,1)S(1)} %copy-done.2, bf16[256,1024]{1,0:T(8,128)(2,1)S(1)} %copy-done.1, ...), custom_call_target="tpu_custom_call" | custom-call | tf_op jit(solution)/shard_map/pallas_call | solution.py:224
  115.3 0.0 copy-start
  115.3 1.0 copy-done
  116.3 7.7 %shard_map.69 = bf16[32,64,1024]{2,1,0:T(8,128)(2,1)} custom-call(s32[32]{0:T(128)} %select_reduce_fusion.selected_ref, bf16[32,64,1024]{2,1,0:T(8,128)(2,1)} %bitcast.8, bf16[8,64,1024]{2,1,0:T(8,128)(2,1)} %copy-done), custom_call_target="tpu_custom_call" | custom-call | tf_op jit(solution)/shard_map/pallas_call | solution.py:255
  124.0 0.7 copy.15
  (3 shorter events, 0.0 us)
Async XLA Ops:
  0.6 19.0 %copy-start.2 = (bf16[256,256]{1,0:T(8,128)(2,1)S(1)}, bf16[256,256]{1,0:T(8,128)(2,1)}, u32[]{:S(2)}) copy-start(bf16[256,256]{1,0:T(8,128)(2,1)} %codes_ref.1) | copy-start | bytes 393220
  0.6 19.0 %copy-start.1 = (bf16[256,1024]{1,0:T(8,128)(2,1)S(1)}, bf16[256,1024]{1,0:T(8,128)(2,1)}, u32[]{:S(2)}) copy-start(bf16[256,1024]{1,0:T(8,128)(2,1)} %patterns_ref.1) | copy-start | bytes 1572868
  2.0 13.7 %all-to-all-start = ((s32[1,8,1]{2,0,1:T(1,128)}), s32[1,8,1]{2,0,1:T(1,128)S(1)}, u32[]{:S(2)}, u32[]{:S(2)}) async-start(s32[1,8,1]{2,0,1:T(1,128)} %copy.12), calls=%async_computation | async-start | bytes 8192 | tf_op jit(solution)/shard_map/all_to_all | solution.py:218
  115.3 1.0 copy-start

commit v2 on v1

--- a/solution.py
+++ b/solution.py
@@ -15,15 +15,27 @@
 
 def steps_kernel(
     owners, row_count, block_width, chunk, scale_factor,
-    same_ref, support_ref, codes_ref, patterns_ref, slots_ref,
-    slots_out, codes_out,
-    panels, arrived, terms, slots_next, dense, correlated, code_parts,
-    send_sems, recv_sems, code_send, code_recv,
+    wanted_ref, support_hbm, codes_hbm, patterns_hbm, dictionary_hbm,
+    dictionary_out, codes_out,
+    support_ref, codes_ref, patterns_ref, pool, asked_vmem, asked_smem, chosen,
+    panels, arrived, terms, slots_before, slots_next, dense, correlated, code_parts,
+    send_sems, recv_sems, code_send, code_recv, ask_send, ask_recv, load_sems,
 ):
     me = lax.axis_index("blk")
     my_row = lax.axis_index("rows")
     pattern_rows, pixel_count = patterns_ref.shape
+    owned_blocks = dictionary_out.shape[0]
     chunks = pixel_count // chunk
+    loads = (
+        pltpu.make_async_copy(
+            dictionary_hbm, pool.at[pl.ds(0, owned_blocks)], load_sems.at[0]
+        ),
+        pltpu.make_async_copy(codes_hbm, codes_ref, load_sems.at[1]),
+        pltpu.make_async_copy(support_hbm, support_ref, load_sems.at[2]),
+        pltpu.make_async_copy(patterns_hbm, patterns_ref, load_sems.at[3]),
+    )
+    for load in loads:
+        load.start()
     support_count = support_ref.shape[1]
     lanes = 128
     per_lane = lanes // block_width
@@ -56,17 +68,54 @@
         for j in range(1, owners):
             block_copy(phase, k, j, target, target).wait_recv()
 
+    def ask_copy(j):
+        return pltpu.make_async_remote_copy(
+            src_ref=wanted_ref,
+            dst_ref=asked_vmem.at[me],
+            send_sem=ask_send.at[j],
+            recv_sem=ask_recv.at[j],
+            device_id={"blk": lax.rem(me + j, owners)},
+            device_id_type=MESH,
+        )
+
+    for j in range(1, owners):
+        ask_copy(j).start()
+    asked_vmem[me] = wanted_ref[...]
+    for j in range(1, owners):
+        ask_copy(j).wait_recv()
+    move = pltpu.make_async_copy(asked_vmem, asked_smem, load_sems.at[4])
+    move.start()
+    move.wait()
+    loads[0].wait()
+
+    def asked(r):
+        return asked_smem[r, 0, me]
+
     def send_panels(k, _):
+        def gather(r, _):
+            slots_before[k, r] = pool[asked(r), :, columns(k)]
+            return 0
+
+        lax.fori_loop(0, owners, gather, 0)
         for j in range(1, owners):
             block_copy(
-                0, k, j,
-                slots_ref.at[lax.rem(me + j, owners), :, columns(k)],
-                panels.at[0, k, me],
+                0, k, j, slots_before.at[k, lax.rem(me + j, owners)], panels.at[0, k, me]
             ).start()
-        panels[0, k, me] = slots_ref[me, :, columns(k)]
+        panels[0, k, me] = slots_before[k, me]
         return 0
 
     lax.fori_loop(0, chunks, send_panels, 0)
+
+    def choose(b, _):
+        place = b
+        for r in range(owners):
+            place = jnp.where(asked(r) == b, owned_blocks + r, place)
+        chosen[b] = place
+        return 0
+
+    lax.fori_loop(0, owned_blocks, choose, 0)
+    for load in loads[1:]:
+        load.wait()
 
     half = lax.broadcasted_iota(jnp.int32, (pattern_rows, lanes), 1) // block_width
 
@@ -150,13 +199,14 @@
             def one_slot(r, _):
                 total = jnp.zeros((block_width, chunk), jnp.float32)
                 for q in range(owners):
-                    total = total + same_ref[r, q] * arrived[step, k, q].astype(jnp.float32)
-                before = slots_ref[r, :, columns(k)] if step == 0 else slots_next[k, r]
+                    same = jnp.where(asked(r) == asked(q), 1.0, 0.0).astype(jnp.float32)
+                    total = total + same * arrived[step, k, q].astype(jnp.float32)
+                before = slots_before[k, r] if step == 0 else slots_next[k, r]
                 after = (before.astype(jnp.float32) + ATOM_RATE * total).astype(jnp.bfloat16)
                 if step == 0:
                     slots_next[k, r] = after
                 else:
-                    slots_out[r, :, columns(k)] = after
+                    pool[owned_blocks + r, :, columns(k)] = after
                 return 0
 
             lax.fori_loop(0, owners, one_slot, 0)
@@ -178,6 +228,12 @@
             total = total + code_parts[step, i].astype(jnp.float32)
         codes_out[...] += CODE_RATE * total
 
+    def place_block(b, _):
+        dictionary_out[b] = pool[chosen[b]]
+        return 0
+
+    lax.fori_loop(0, owned_blocks, place_block, 0)
+
     def drain(k, _):
         for phase in range(4):
             for j in range(1, owners):
@@ -188,20 +244,8 @@
     for step in range(2):
         for j in range(1, row_count):
             code_copy(step, j).wait_send()
-
-
-def put_kernel(group, selected_ref, dictionary_ref, slots_ref, out_ref):
-    first = pl.program_id(0) * group
-    for i in range(group):
-        chosen = selected_ref[first + i]
-
-        @pl.when(chosen >= 0)
-        def _():
-            out_ref[i] = slots_ref[jnp.maximum(chosen, 0)]
-
-        @pl.when(chosen < 0)
-        def _():
-            out_ref[i] = dictionary_ref[i]
+    for j in range(1, owners):
+        ask_copy(j).wait_send()
 
 
 def local(patterns, dictionary, codes, support, wanted):
@@ -215,24 +259,30 @@
     scale_factor = code_width ** (-0.5)
     chunk = min(CHUNK, pixel_count)
     chunks = pixel_count // chunk
-    asked = lax.all_to_all(wanted, "blk", split_axis=1, concat_axis=0, tiled=True)[:, 0]
-    same = (asked[:, None] == asked[None, :]).astype(jnp.float32)
     blocks = dictionary.reshape(owned_blocks, block_width, pixel_count)
-    slots = jnp.take(blocks, asked, axis=0)
     vmem = pl.BlockSpec(memory_space=pltpu.VMEM)
     bf16 = jnp.bfloat16
-    slots_after, codes_after = pl.pallas_call(
+    hbm = pl.BlockSpec(memory_space=pl.ANY)
+    dictionary_after, codes_after = pl.pallas_call(
         functools.partial(steps_kernel, owners, row_count, block_width, chunk, scale_factor),
         out_shape=(
-            jax.ShapeDtypeStruct((owners, block_width, pixel_count), bf16),
+            jax.ShapeDtypeStruct((owned_blocks, block_width, pixel_count), bf16),
             jax.ShapeDtypeStruct((pattern_rows, code_width), jnp.float32),
         ),
-        in_specs=[pl.BlockSpec(memory_space=pltpu.SMEM)] + [vmem] * 4,
+        in_specs=[vmem] + [hbm] * 4,
         out_specs=(vmem, vmem),
         scratch_shapes=[
+            pltpu.VMEM(support.shape, jnp.int32),
+            pltpu.VMEM(codes.shape, bf16),
+            pltpu.VMEM(patterns.shape, bf16),
+            pltpu.VMEM((owned_blocks + owners, block_width, pixel_count), bf16),
+            pltpu.VMEM((owners,) + wanted.shape, jnp.int32),
+            pltpu.SMEM((owners,) + wanted.shape, jnp.int32),
+            pltpu.SMEM((owned_blocks,), jnp.int32),
             pltpu.VMEM((2, chunks, owners, block_width, chunk), bf16),
             pltpu.VMEM((2, chunks, owners, block_width, chunk), bf16),
             pltpu.VMEM((2, chunks, owners, block_width, chunk), bf16),
+            pltpu.VMEM((chunks, owners, block_width, chunk), bf16),
             pltpu.VMEM((chunks, owners, block_width, chunk), bf16),
             pltpu.VMEM((pattern_rows, owners * block_width), bf16),
             pltpu.VMEM((pattern_rows, owners * block_width), jnp.float32),
@@ -241,30 +291,14 @@
             pltpu.SemaphoreType.DMA((4, chunks, owners)),
             pltpu.SemaphoreType.DMA((2, row_count)),
             pltpu.SemaphoreType.DMA((2, row_count)),
+            pltpu.SemaphoreType.DMA((owners,)),
+            pltpu.SemaphoreType.DMA((owners,)),
+            pltpu.SemaphoreType.DMA((5,)),
         ],
         compiler_params=pltpu.CompilerParams(
             collective_id=0, has_side_effects=True, vmem_limit_bytes=40 * 1024 * 1024
         ),
-    )(same, support, codes, patterns, slots)
-    slot_ids = jnp.arange(owners, dtype=jnp.int32)
-    block_ids = jnp.arange(owned_blocks, dtype=jnp.int32)
-    selected = jnp.max(
-        jnp.where(asked[None, :] == block_ids[:, None], slot_ids[None, :], -1), axis=1
-    )
-    group = 4
-    dictionary_after = pl.pallas_call(
-        functools.partial(put_kernel, group),
-        out_shape=jax.ShapeDtypeStruct(blocks.shape, bf16),
-        grid_spec=pltpu.PrefetchScalarGridSpec(
-            num_scalar_prefetch=1,
-            grid=(owned_blocks // group,),
-            in_specs=[
-                pl.BlockSpec((group, block_width, pixel_count), lambda i, sel: (i, 0, 0)),
-                pl.BlockSpec((owners, block_width, pixel_count), lambda i, sel: (0, 0, 0)),
-            ],
-            out_specs=pl.BlockSpec((group, block_width, pixel_count), lambda i, sel: (i, 0, 0)),
-        ),
-    )(selected, blocks, slots_after)
+    )(wanted, support, codes, patterns, blocks)
     return (dictionary_after.reshape(dictionary.shape), codes_after)
 
 

time: 125 us -> 114 us (0.912)
  starting transfers between devices: 7.28 us -> 0 us
  waiting for transfers between devices: 5.6 us -> 0 us
  Pallas kernels: 103 us -> 105 us
  local copies, waits for them, and re-layouts: 6.69 us -> 8.32 us
    pallas_call x1, Pallas kernels: 95.6 us -> 105 us  [local(): pl.pallas_call(functools.partial(steps_kernel, owners, row_count, block_w...]
    pallas_call x1 -> x0, Pallas kernels: 7.69 us -> none  [local(): pl.pallas_call(functools.partial(put_kernel, group), out_shape=jax.ShapeD...]
    all_to_all x1 -> x0, starting transfers between devices: 7.28 us -> none  [local(): lax.all_to_all(wanted, 'blk', split_axis=1, concat_axis=0, tiled=True)[:, 0]]
    unnamed x8 -> x11, local copies, waits for them, and re-layouts: 2.5 us -> 8.32 us
    all_to_all x1 -> x0, waiting for transfers between devices: 5.6 us -> none  [local(): lax.all_to_all(wanted, 'blk', split_axis=1, concat_axis=0, tiled=True)[:, 0]]
    gather x1 -> x0, local copies, waits for them, and re-layouts: 2.8 us -> none  [local(): slots = jnp.take(blocks, asked, axis=0)]
    all_to_all x1 -> x0, local copies, waits for them, and re-layouts: 1.39 us -> none  [local(): lax.all_to_all(wanted, 'blk', split_axis=1, concat_axis=0, tiled=True)[:, 0]]
  transfers between devices with their start and end apart: 1 -> 0, of which waited for: 1 -> 0; matrix products, arithmetic and copies ran while one was open for 1% -> 0% of each run, Pallas kernels for 0% -> 0%
where the time goes in v2:
time: 114 us
  Pallas kernels  105 us (92%)
  local copies, waits for them, and re-layouts  8.32 us (7%)
    pallas_call x1, Pallas kernels, local(): pl.pallas_call(functools.partial(steps_kernel, owners, row_count, block_w...  105 us
    unnamed x11, local copies, waits for them, and re-layouts  8.32 us

profile of v2, /device:TPU:0, one launch (start us, length us, event | category | flops | bytes accessed | tf_op | source)
XLA Modules:
  0.0 114.0 jit_solution(8137490728163074350)
XLA Ops:
  0.6 0.8 copy.7.support_hbm
  1.5 0.0 copy-start
  1.5 2.2 %copy-done = bf16[2048,1024]{1,0:T(8,128)(2,1)S(1)} copy-done((bf16[2048,1024]{1,0:T(8,128)(2,1)S(1)}, bf16[2048,1024]{1,0:T(8,128)(2,1)}, u32[]{:S(2)}) %copy-start) | copy-done | bytes 4194328
  3.6 0.0 copy-start.1
  3.6 1.0 copy-done.1
  4.7 0.0 copy-start.2
  4.7 0.9 copy-done.2
  5.6 0.0 copy-start.3
  5.6 0.7 copy-done.3
  6.2 105.0 %shard_map.68 = (bf16[32,64,1024]{2,1,0:T(8,128)(2,1)S(1)}, f32[256,256]{1,0:T(8,128)S(1)}) custom-call(s32[1,8]{1,0:T(1,128)S(1)} %copy-done.3, s32[256,4]{1,0:T(8,128)S(1)} %copy.7.support_hbm, bf16[256,256]{1,0:T(8,128)(2,1)S(1)} %copy-done.2, bf16[256,1024]{1,0:T(8,128)(2,1)S(1)} %copy-done.1, bf16[32,64,1024]{2,1,0:T(8,128)(2,1)S(1)} %bitcast.2), custom_call_target="tpu_custom_call" | custom-call | tf_op jit(solution)/shard_map/pallas_call | solution.py:266
  111.3 2.0 %copy.10 = bf16[2048,1024]{1,0:T(8,128)(2,1)} copy(bf16[2048,1024]{1,0:T(8,128)(2,1)S(1)} %bitcast.3) | data formatting | bytes 8388608
  113.3 0.7 copy.11
Async XLA Ops:
  1.5 2.2 %copy-start = (bf16[2048,1024]{1,0:T(8,128)(2,1)S(1)}, bf16[2048,1024]{1,0:T(8,128)(2,1)}, u32[]{:S(2)}) copy-start(bf16[2048,1024]{1,0:T(8,128)(2,1)} %param.6) | copy-start | bytes 12582916
  3.6 1.0 copy-start.1
  4.7 0.9 copy-start.2
  5.6 0.7 copy-start.3

commit v3 on v2

--- a/solution.py
+++ b/solution.py
@@ -296,7 +296,7 @@
             pltpu.SemaphoreType.DMA((5,)),
         ],
         compiler_params=pltpu.CompilerParams(
-            collective_id=0, has_side_effects=True, vmem_limit_bytes=40 * 1024 * 1024
+            collective_id=0, has_side_effects=True, vmem_limit_bytes=60 * 1024 * 1024
         ),
     )(wanted, support, codes, patterns, blocks)
     return (dictionary_after.reshape(dictionary.shape), codes_after)

time: 114 us -> 115 us (level)
  Pallas kernels: 105 us -> 107 us
  local copies, waits for them, and re-layouts: 8.32 us -> 6.87 us
    pallas_call x1, Pallas kernels: 105 us -> 107 us  [local(): pl.pallas_call(functools.partial(steps_kernel, owners, row_count, block_w...]
    unnamed x11 -> x5, local copies, waits for them, and re-layouts: 8.32 us -> 6.87 us
where the time goes in v3:
time: 115 us
  Pallas kernels  107 us (93%)
  local copies, waits for them, and re-layouts  6.87 us (6%)
    pallas_call x1, Pallas kernels, local(): pl.pallas_call(functools.partial(steps_kernel, owners, row_count, block_w...  107 us
    unnamed x5, local copies, waits for them, and re-layouts  6.87 us

profile of v3, /device:TPU:0, one launch (start us, length us, event | category | flops | bytes accessed | tf_op | source)
XLA Modules:
  0.0 114.6 jit_solution(5453257205397374863)
XLA Ops:
  0.6 1.5 %copy.7.support_hbm = s32[256,4]{1,0:T(8,128)} copy(s32[256,4]{0,1:T(4,128)} %param.8) | data formatting | bytes 8192 | tf_op args[3]
  2.1 107.1 %shard_map.68 = (bf16[32,64,1024]{2,1,0:T(8,128)(2,1)}, f32[256,256]{1,0:T(8,128)}) custom-call(s32[1,8]{1,0:T(1,128)} %wanted_ref.1, s32[256,4]{1,0:T(8,128)} %copy.7.support_hbm, bf16[256,256]{1,0:T(8,128)(2,1)} %codes_hbm.1, bf16[256,1024]{1,0:T(8,128)(2,1)} %patterns_hbm.1, bf16[32,64,1024]{2,1,0:T(8,128)(2,1)} %bitcast.2), custom_call_target="tpu_custom_call" | custom-call | tf_op jit(solution)/shard_map/pallas_call | solution.py:266
  109.2 0.0 copy-start
  109.2 4.7 %copy.10 = bf16[2048,1024]{1,0:T(8,128)(2,1)} copy(bf16[2048,1024]{1,0:T(8,128)(2,1)} %bitcast.3) | data formatting | bytes 8388608
  113.9 0.0 copy-done
  113.9 0.7 copy.11
Async XLA Ops:
  109.2 4.7 %copy-start = (f32[256,256]{1,0:T(8,128)S(1)}, f32[256,256]{1,0:T(8,128)}, u32[]{:S(2)}) copy-start(f32[256,256]{1,0:T(8,128)} %get-tuple-element.9) | copy-start | bytes 786436

commit v4 on v3

--- a/solution.py
+++ b/solution.py
@@ -36,7 +36,7 @@
     )
     for load in loads:
         load.start()
-    support_count = support_ref.shape[1]
+    support_count = support_ref.shape[0]
     lanes = 128
     per_lane = lanes // block_width
 
@@ -114,13 +114,14 @@
         return 0
 
     lax.fori_loop(0, owned_blocks, choose, 0)
+
     for load in loads[1:]:
         load.wait()
-
+    support_now = support_ref[...].T
     half = lax.broadcasted_iota(jnp.int32, (pattern_rows, lanes), 1) // block_width
 
     def matches(s, m):
-        return support_ref[:, s:s + 1] == half + m * per_lane
+        return support_now[:, s:s + 1] == half + m * per_lane
 
     def spread(codes_now):
         pieces = []
@@ -262,7 +263,7 @@
     blocks = dictionary.reshape(owned_blocks, block_width, pixel_count)
     vmem = pl.BlockSpec(memory_space=pltpu.VMEM)
     bf16 = jnp.bfloat16
-    hbm = pl.BlockSpec(memory_space=pl.ANY)
+    hbm = pl.BlockSpec(memory_space=pltpu.HBM)
     dictionary_after, codes_after = pl.pallas_call(
         functools.partial(steps_kernel, owners, row_count, block_width, chunk, scale_factor),
         out_shape=(
@@ -272,7 +273,7 @@
         in_specs=[vmem] + [hbm] * 4,
         out_specs=(vmem, vmem),
         scratch_shapes=[
-            pltpu.VMEM(support.shape, jnp.int32),
+            pltpu.VMEM(support.shape[::-1], jnp.int32),
             pltpu.VMEM(codes.shape, bf16),
             pltpu.VMEM(patterns.shape, bf16),
             pltpu.VMEM((owned_blocks + owners, block_width, pixel_count), bf16),
@@ -296,9 +297,9 @@
             pltpu.SemaphoreType.DMA((5,)),
         ],
         compiler_params=pltpu.CompilerParams(
-            collective_id=0, has_side_effects=True, vmem_limit_bytes=60 * 1024 * 1024
+            collective_id=0, has_side_effects=True, vmem_limit_bytes=47 * 1024 * 1024
         ),
-    )(wanted, support, codes, patterns, blocks)
+    )(wanted, support.T, codes, patterns, blocks)
     return (dictionary_after.reshape(dictionary.shape), codes_after)
 
 

time: 115 us -> 111 us (0.965)
  Pallas kernels: 107 us -> 105 us
    pallas_call x1, Pallas kernels: 107 us -> 105 us  [local(): pl.pallas_call(functools.partial(steps_kernel, owners, row_count, block_w...]
    unnamed x5 -> x10, local copies, waits for them, and re-layouts: 6.87 us -> 6 us
where the time goes in v4:
time: 111 us
  Pallas kernels  105 us (95%)
  local copies, waits for them, and re-layouts  6 us (5%)
    pallas_call x1, Pallas kernels, local(): pl.pallas_call(functools.partial(steps_kernel, owners, row_count, block_w...  105 us
    unnamed x10, local copies, waits for them, and re-layouts  6 us

profile of v4, /device:TPU:0, one launch (start us, length us, event | category | flops | bytes accessed | tf_op | source)
XLA Modules:
  0.0 111.2 jit_solution(8681805364436937023)
XLA Ops:
  0.6 0.0 copy-start
  0.6 1.0 copy-done
  1.7 0.0 copy-start.1
  1.7 0.9 copy-done.1
  2.6 0.0 copy-start.2
  2.6 0.7 copy-done.2
  3.3 0.0 copy-start.3
  3.3 0.7 copy-done.3
  3.9 104.5 %shard_map.68 = (bf16[32,64,1024]{2,1,0:T(8,128)(2,1)S(1)}, f32[256,256]{1,0:T(8,128)S(1)}) custom-call(s32[1,8]{1,0:T(1,128)S(1)} %copy-done.3, s32[4,256]{1,0:T(4,128)S(1)} %bitcast.4, bf16[256,256]{1,0:T(8,128)(2,1)S(1)} %copy-done.1, bf16[256,1024]{1,0:T(8,128)(2,1)S(1)} %copy-done, bf16[32,64,1024]{2,1,0:T(8,128)(2,1)} %bitcast.5), custom_call_target="tpu_custom_call" | custom-call | tf_op jit(solution)/shard_map/pallas_call | solution.py:267
  108.5 2.0 %copy.9 = bf16[2048,1024]{1,0:T(8,128)(2,1)} copy(bf16[2048,1024]{1,0:T(8,128)(2,1)S(1)} %bitcast.3) | data formatting | bytes 8388608
  110.5 0.7 copy.10
Async XLA Ops:
  0.6 1.0 copy-start
  1.7 0.9 copy-start.1
  2.6 0.7 copy-start.2
  3.3 0.7 copy-start.3
